TPU v7x, 32 devices: a whole 2x2x4 slice. The times are simulated.
32 devices in a mesh: group: 2 (over x), src: 16 (over z, y, core).
Axes of the slice: x: 2, y: 2, z: 4, core: 2. Of those that a mesh axis runs over, the one named last changes fastest.
Arguments:
- positions: float32 [2, 32768], P(None, ('group', 'src')), parts along dimension 1, may hold values from -0.2 to 0.2
- flux: float32 [4, 32768], P(None, ('group', 'src')), parts along dimension 1, may hold values from 0.1 to 2
- cluster: int32 [32768], P(('group', 'src')), parts along dimension 0, may hold values from 0 to 15
- jones: float32 [4, 2, 16, 1024], P(None, None, None, ('group', 'src')), parts along dimension 3, may hold values from -4 to 4
- station_uvw: float32 [3, 1024], P(None, ('group', 'src')), parts along dimension 1, may hold values from -600 to 600
- channels: int32 [8], P('group'), parts along dimension 0, may hold values from 0 to 383
- tile_map: int32 [32, 2], P('group'), parts along dimension 0, may hold values from 0 to 15, as said below
Outputs:
- visibilities: float32 [32, 4, 2, 1024], P(('group', 'src')), parts along dimension 0
There are 2 independent parts, one for each index of `group`. A program takes and returns all parts, laid end to end along the dimension named above; each array names one. Nothing has to cross between parts.
Inputs may be any that keep to these rules, and one draw needn't show every extreme that they name: `tile_map`: each row is a pair of station tiles (first, second) with first <= second; the 16 pairs are distinct.
All inputs are finite; a program needn't handle non-finite values.
Results may differ from a plain program's by a relative error of at most 0.0038.
Values sent between devices are 32-bit elements; how exact they have to be, the bound alone decides.
A program may use at most 128 MiB of HBM per device.

v0:
```python
import functools
import math

import jax
import jax.numpy as jnp
from jax import lax
from jax.experimental import pallas as pl
from jax.experimental.pallas import tpu as pltpu
from jax.sharding import PartitionSpec as P

MESH = pl.DeviceIdType.MESH
TS = 32
GROUP = 64
HALF = 48
CHUNK = 256
SINE = (3.1415820121765137, -5.167142868041992, 2.5418992042541504, -0.5546366572380066)
ATAN = (
    0.15915492177009583,
    -0.05305047705769539,
    0.031808558851480484,
    -0.022538291290402412,
    0.016709571704268456,
    -0.011514591053128242,
    0.006331328768283129,
    -0.0022920165210962296,
    0.00039099203422665596,
)
ONE = 1.0 + 6e-7


def horner(coefs, y):
    total = jnp.float32(coefs[-1])
    for coef in coefs[-2::-1]:
        total = total * y + jnp.float32(coef)
    return total


def three_parts(value):
    first = value.astype(jnp.bfloat16).astype(jnp.float32)
    rest = value - first
    second = rest.astype(jnp.bfloat16).astype(jnp.float32)
    return first, second, rest - second


def polar(real, imag):
    wide, tall = jnp.abs(real), jnp.abs(imag)
    large, small = jnp.maximum(wide, tall), jnp.minimum(wide, tall)
    ratio = small / jnp.where(large > 0.0, large, 1.0)
    square = ratio * ratio
    size = large * jnp.sqrt(1.0 + square)
    angle = ratio * horner(ATAN, square)
    angle = jnp.where(tall > wide, 0.25 - angle, angle)
    angle = jnp.where(real < 0.0, 0.5 - angle, angle)
    return size, jnp.where(imag < 0.0, -angle, angle)


def kernel(
    devices,
    chans,
    dirs,
    scale,
    tile_ref,
    channel_ref,
    position_ref,
    flux_ref,
    cluster_ref,
    jones_ref,
    uvw_ref,
    out_ref,
    stations,
    sources,
    table,
    onehots,
    sides,
    acc,
    st_send,
    st_recv,
    st_fwd_send,
    st_fwd_recv,
    so_send,
    so_recv,
    so_fwd_send,
    so_fwd_recv,
):
    chips = devices // 2
    me = lax.axis_index("src")
    chip = me // 2
    core = lax.rem(me, 2)
    partner = chip * 2 + 1 - core
    rows = stations.shape[1]
    per_dev = rows * 2 // chans
    width = sources.shape[2]

    barrier = pltpu.get_barrier_semaphore()

    def greet(k, carry):
        there = lax.rem(chip + k, chips) * 2 + core
        pl.semaphore_signal(barrier, inc=1, device_id={"src": there}, device_id_type=MESH)
        return carry

    pl.semaphore_signal(barrier, inc=1, device_id={"src": partner}, device_id_type=MESH)
    lax.fori_loop(1, chips, greet, 0)

    l_own, m_own = position_ref[0:1, :], position_ref[1:2, :]
    sources[me, 0:2, :] = position_ref[...]
    sources[me, 2 : 2 + chans, :] = flux_ref[...]
    sources[me, 2 + chans : 3 + chans, :] = cluster_ref[...].astype(jnp.float32)
    sources[me, 3 + chans : 4 + chans, :] = jnp.sqrt(1.0 - l_own * l_own - m_own * m_own) - 1.0
    eight = lax.broadcasted_iota(jnp.int32, (8, per_dev), 0)
    coords = jnp.where(eight == 0, uvw_ref[0:1, :], 0.0)
    coords = jnp.where(eight == 1, uvw_ref[1:2, :], coords)
    coords = jnp.where(eight == 3 + chans, uvw_ref[2:3, :], coords)
    for pair in range(chans // 2):
        features = []
        for c in (2 * pair, 2 * pair + 1):
            freq_ratio = 1.0 + 0.002 * channel_ref[c].astype(jnp.float32)
            size, angle = polar(jones_ref[c, 0], jones_ref[c, 1])
            shifted = coords * freq_ratio
            features += [-angle, shifted, shifted, shifted]
            features += [jnp.zeros((HALF - dirs - 24, per_dev), jnp.float32), 2.0 * size]
        stations[me, pair * per_dev : (pair + 1) * per_dev, :] = jnp.concatenate(features, 0).T

    pl.semaphore_wait(barrier, chips)

    def direct(mine, slots, send, recv, k):
        there = lax.rem(chip + k, chips) * 2 + core
        return pltpu.make_async_remote_copy(
            src_ref=mine,
            dst_ref=slots.at[me],
            send_sem=send.at[k],
            recv_sem=recv.at[k],
            device_id={"src": there},
            device_id_type=MESH,
        )

    def arrival(mine, slots, send, recv, k):
        came = lax.rem(chip - k + chips, chips) * 2 + core
        return pltpu.make_async_remote_copy(
            src_ref=mine,
            dst_ref=slots.at[came],
            send_sem=send.at[k],
            recv_sem=recv.at[k],
            device_id={"src": partner},
            device_id_type=MESH,
        )

    def forward(slots, send, recv, k):
        came = lax.rem(chip - k + chips, chips) * 2 + core
        return pltpu.make_async_remote_copy(
            src_ref=slots.at[came],
            dst_ref=slots.at[came],
            send_sem=send.at[k],
            recv_sem=recv.at[k],
            device_id={"src": partner},
            device_id_type=MESH,
        )

    def forwarded(slots, send, recv, k):
        came = lax.rem(chip - k + chips, chips) * 2 + 1 - core
        return pltpu.make_async_remote_copy(
            src_ref=slots.at[came],
            dst_ref=slots.at[came],
            send_sem=send.at[k],
            recv_sem=recv.at[k],
            device_id={"src": partner},
            device_id_type=MESH,
        )

    forward(stations, st_fwd_send, st_fwd_recv, 0).start()

    def send_stations(k, carry):
        direct(stations.at[me], stations, st_send, st_recv, k).start()
        return carry

    lax.fori_loop(1, chips, send_stations, 0)
    forward(sources, so_fwd_send, so_fwd_recv, 0).start()

    def send_sources(k, carry):
        direct(sources.at[me], sources, so_send, so_recv, k).start()
        return carry

    lax.fori_loop(1, chips, send_sources, 0)

    onehots[:, 3 * GROUP :, :] = jnp.zeros((2, GROUP, width), jnp.bfloat16)
    sides[1] = jnp.zeros(sides.shape[1:], jnp.bfloat16)
    acc[...] = jnp.zeros_like(acc)

    def relay_stations(k, carry):
        arrival(stations.at[me], stations, st_send, st_recv, k).wait_recv()
        forward(stations, st_fwd_send, st_fwd_recv, k).start()
        return carry

    lax.fori_loop(1, chips, relay_stations, 0)

    def take_stations(k, carry):
        forwarded(stations, st_fwd_send, st_fwd_recv, k).wait_recv()
        return carry

    lax.fori_loop(0, chips, take_stations, 0)

    per_tile = TS // per_dev
    lane = lax.broadcasted_iota(jnp.int32, (TS, 128), 1)
    is_phase = lax.rem(lane, GROUP) < HALF
    low = lane < GROUP
    half_rows = chans * TS
    tiles = [tile_ref[me, 0], tile_ref[me, 1]]
    for side in range(2):
        held = [stations[tiles[side] * per_tile + d] for d in range(per_tile)]
        for c in range(chans):
            begin = c // 2 * per_dev
            value = jnp.concatenate([part[begin : begin + per_dev] for part in held], 0)
            if c % 2:
                value = pltpu.roll(value, GROUP, 1)
            value = jnp.where(low, value, 0.0)
            first, second, third = three_parts(value)
            pieces = [first + pltpu.roll(second, GROUP, 1), third]
            at = (side * chans + c) * 2 * TS
            for index, piece in enumerate(pieces):
                cols = slice(index * 128, index * 128 + 128)
                table[at : at + TS, cols] = jnp.where(is_phase, piece, 0.0).astype(jnp.bfloat16)
                below = at + TS
                table[below : below + TS, cols] = jnp.where(is_phase, 0.0, piece).astype(
                    jnp.bfloat16
                )

    contract = (((1,), (1,)), ((), ()))

    def predict(slot, came):
        rows_in = sources[came]
        kinds = rows_in[2 + chans : 3 + chans, :]
        parts = three_parts(rows_in) + (jnp.zeros_like(rows_in),)
        kind_rows = lax.broadcasted_iota(jnp.int32, (dirs, width), 0).astype(jnp.float32)
        onehot = jnp.where(kind_rows == kinds, 1.0, 0.0).astype(jnp.bfloat16)
        upper = jnp.concatenate(parts[:2], 0).astype(jnp.bfloat16)
        lower = jnp.concatenate(parts[2:], 0).astype(jnp.bfloat16)
        for part in range(3):
            base = part * GROUP
            for index, value in enumerate((onehot, upper, lower, onehot)):
                onehots[slot, base + index * 16 : base + index * 16 + 16, :] = value

        for chunk in range(width // CHUNK):
            cols = slice(chunk * CHUNK, chunk * CHUNK + CHUNK)
            weights = onehots[slot, :, cols]
            found = jnp.dot(table[...], weights, preferred_element_type=jnp.float32)
            for side in range(2):
                for c in range(chans):
                    at = (side * chans + c) * 2 * TS
                    turns = found[at : at + TS]
                    double = found[at + TS : at + 2 * TS]
                    if side == 0:
                        double = double * (sources[came, 2 + c : 3 + c, cols] * scale)
                    turns = turns - jnp.round(turns)
                    sine = turns * horner(SINE, turns * turns)
                    square = sine * sine
                    rest = ONE - square
                    cosine = rest * lax.rsqrt(rest)
                    real = double * (0.5 - square)
                    imag = (double * sine) * cosine
                    top = c * TS
                    sides[slot, side, top : top + TS, cols] = real.astype(jnp.bfloat16)
                    sides[slot, side, half_rows + top : half_rows + top + TS, cols] = imag.astype(
                        jnp.bfloat16
                    )

    def add_products(slot):
        acc[...] += lax.dot_general(
            sides[slot, 0], sides[slot, 1], contract, preferred_element_type=jnp.float32
        )

    def step(k, carry):
        came = lax.rem(chip - k + chips, chips) * 2
        predict(0, came + core)
        add_products(1)

        @pl.when(k + 1 < chips)
        def _():
            arrival(sources.at[me], sources, so_send, so_recv, k + 1).wait_recv()
            forward(sources, so_fwd_send, so_fwd_recv, k + 1).start()

        forwarded(sources, so_fwd_send, so_fwd_recv, k).wait_recv()
        predict(1, came + 1 - core)
        add_products(0)
        return carry

    lax.fori_loop(0, chips, step, 0)
    add_products(1)

    same = tiles[0] == tiles[1]
    diagonal = lax.broadcasted_iota(jnp.int32, (TS, TS), 0) == lax.broadcasted_iota(
        jnp.int32, (TS, TS), 1
    )
    clear = jnp.logical_and(diagonal, same)
    for c in range(chans):
        top = slice(c * TS, c * TS + TS)
        low_rows = slice(half_rows + c * TS, half_rows + c * TS + TS)
        real_rows = acc[top, :]
        imag_rows = acc[low_rows, :]
        real = real_rows[:, top] + imag_rows[:, low_rows]
        imag = real_rows[:, low_rows] - imag_rows[:, top]
        for part, value in enumerate((real, imag)):
            value = jnp.where(clear, 0.0, value)
            for i in range(TS):
                out_ref[0, c, part : part + 1, i * TS : i * TS + TS] = value[i : i + 1, :]

    def finish(k, carry):
        direct(stations.at[me], stations, st_send, st_recv, k).wait_send()
        direct(sources.at[me], sources, so_send, so_recv, k).wait_send()
        return carry

    lax.fori_loop(1, chips, finish, 0)

    def finish_forward(k, carry):
        forward(stations, st_fwd_send, st_fwd_recv, k).wait_send()
        forward(sources, so_fwd_send, so_fwd_recv, k).wait_send()
        return carry

    lax.fori_loop(0, chips, finish_forward, 0)


def on_device(positions, flux, cluster, jones, station_uvw, channels, tile_map):
    width = positions.shape[1]
    devices = lax.axis_size("src")
    scale = 1.0 / math.sqrt(width * devices)
    chans, _, dirs, per_dev = jones.shape

    wide = 2 * chans * TS
    chips = devices // 2
    vmem = pl.BlockSpec(memory_space=pltpu.VMEM)
    return pl.pallas_call(
        functools.partial(kernel, devices, chans, dirs, scale),
        out_shape=jax.ShapeDtypeStruct((1, chans, 2, TS * TS), jnp.float32),
        in_specs=[pl.BlockSpec(memory_space=pltpu.SMEM)] * 2 + [vmem] * 5,
        out_specs=vmem,
        scratch_shapes=[
            pltpu.VMEM((devices, chans // 2 * per_dev, 2 * GROUP), jnp.float32),
            pltpu.VMEM((devices, 8, width), jnp.float32),
            pltpu.VMEM((2 * wide, 4 * GROUP), jnp.bfloat16),
            pltpu.VMEM((2, 4 * GROUP, width), jnp.bfloat16),
            pltpu.VMEM((2, 2, wide, width), jnp.bfloat16),
            pltpu.VMEM((wide, wide), jnp.float32),
        ]
        + [pltpu.SemaphoreType.DMA((chips,))] * 8,
        compiler_params=pltpu.CompilerParams(collective_id=0, has_side_effects=True),
    )(tile_map, channels, positions, flux, cluster[None], jones, station_uvw)


def solution(mesh):
    in_specs = (
        P(None, ("group", "src")),
        P(None, ("group", "src")),
        P(("group", "src")),
        P(None, None, None, ("group", "src")),
        P(None, ("group", "src")),
        P("group"),
        P("group", None),
    )
    out_specs = P(("group", "src"), None, None, None)
    return jax.shard_map(
        on_device, mesh=mesh, in_specs=in_specs, out_specs=out_specs, check_vma=False
    )
```

profile of v0, /device:TPU:29, one launch (start us, length us, event | category | flops | bytes accessed | tf_op | source)
XLA Modules:
  0.0 35.9 jit_solution(2702561741440790872)
XLA Ops:
  0.0 0.0 copy-start
  0.0 0.7 %copy-done = s32[16,2]{0,1:T(2,128)S(1)} copy-done((s32[16,2]{0,1:T(2,128)S(1)}, s32[16,2]{0,1:T(2,128)}, u32[]{:S(2)}) %copy-start) | copy-done | bytes 152
  0.7 0.7 %copy.8.tile_ref = s32[16,2]{1,0:T(8,128)} copy(s32[16,2]{0,1:T(2,128)S(1)} %copy-done) | data formatting | bytes 256 | tf_op args[6]
  1.4 33.2 %shard_map.73 = f32[1,4,2,1024]{3,2,1,0:T(2,128)} custom-call(s32[16,2]{1,0:T(8,128)} %copy.8.tile_ref, s32[4]{0:T(128)} %channel_ref.1, f32[2,1024]{1,0:T(2,128)} %position_ref.1, f32[4,1024]{1,0:T(4,128)} %flux_ref.1, s32[1,1024]{1,0:T(1,128)} %bitcast.1, f32[4,2,16,32]{3,2,1,0:T(8,128)} %jones_ref.1, f32[3,32]{1,0:T(4,128)} %uvw_ref.1), custom_call_target="tpu_custom_call" | custom-call | tf_op jit(solution)/shard_map/pallas_call | solution.py:329
  34.5 1.4 %copy.10 = f32[1,4,2,1024]{3,2,1,0:T(2,128)} copy(f32[1,4,2,1024]{3,2,1,0:T(2,128)} %shard_map.73) | data formatting | bytes 65536
Async XLA Ops:
  0.0 0.7 %copy-start = (s32[16,2]{0,1:T(2,128)S(1)}, s32[16,2]{0,1:T(2,128)}, u32[]{:S(2)}) copy-start(s32[16,2]{0,1:T(2,128)} %param.13) | copy-start | bytes 388
where the time goes:
time: 36.2 us; the launch traced here: 35.9 us
  Pallas kernels  33.2 us (92%)
  local copies, waits for them, and re-layouts  2.73 us (8%)
    pallas_call x1, Pallas kernels, on_device(): pl.pallas_call(functools.partial(kernel, devices, chans, dirs, scale), ou...  33.2 us
    unnamed x4, local copies, waits for them, and re-layouts  2.73 us

commit v1 on v0

v1 whole, which is shorter than its diff:
```python
import functools
import math

import jax
import jax.numpy as jnp
from jax import lax
from jax.experimental import pallas as pl
from jax.experimental.pallas import tpu as pltpu
from jax.sharding import PartitionSpec as P

MESH = pl.DeviceIdType.MESH
TS = 32
ROWS = 128
CHUNK = 256
SINE = (3.1415820121765137, -5.167142868041992, 2.5418992042541504, -0.5546366572380066)
LEAD = SINE[-1]
MONIC = tuple(coef / LEAD for coef in SINE[:-1])
ATAN = (
    0.15915492177009583,
    -0.05305047705769539,
    0.031808558851480484,
    -0.022538291290402412,
    0.016709571704268456,
    -0.011514591053128242,
    0.006331328768283129,
    -0.0022920165210962296,
    0.00039099203422665596,
)
ONE = (1.0 + 6e-7) / (LEAD * LEAD)
HALF = 0.5 / (LEAD * LEAD)


def horner(coefs, y):
    total = jnp.float32(coefs[-1])
    for coef in coefs[-2::-1]:
        total = total * y + jnp.float32(coef)
    return total


def three_parts(value):
    first = value.astype(jnp.bfloat16).astype(jnp.float32)
    rest = value - first
    second = rest.astype(jnp.bfloat16).astype(jnp.float32)
    return first, second, rest - second


def polar(real, imag):
    wide, tall = jnp.abs(real), jnp.abs(imag)
    large, small = jnp.maximum(wide, tall), jnp.minimum(wide, tall)
    ratio = small / jnp.where(large > 0.0, large, 1.0)
    square = ratio * ratio
    size = large * jnp.sqrt(1.0 + square)
    angle = ratio * horner(ATAN, square)
    angle = jnp.where(tall > wide, 0.25 - angle, angle)
    angle = jnp.where(real < 0.0, 0.5 - angle, angle)
    return size, jnp.where(imag < 0.0, -angle, angle)


def nearest_first(own, step, count):
    spare = count - 1 - own
    reach = jnp.minimum(own, spare)
    half = (step + 1) // 2
    near = own + jnp.where(lax.rem(step, 2) == 1, -half, half)
    return jnp.where(step <= 2 * reach, near, jnp.where(own < spare, step, count - 1 - step))


def kernel(
    devices,
    chans,
    dirs,
    scale,
    tile_ref,
    channel_ref,
    position_ref,
    flux_ref,
    cluster_ref,
    jones_ref,
    uvw_ref,
    out_ref,
    st_send,
    st_recv,
    so_send,
    so_recv,
    table,
    feats,
    plain,
    weighted,
    rs_send,
    rs_recv,
    st_sent,
    st_came,
    so_sent,
    so_came,
    rs_sent,
    rs_came,
):
    me = lax.axis_index("src")
    rank = lax.rem(me, chans)
    planes = devices // chans
    plane = me // chans
    width = position_ref.shape[1]
    per_dev = uvw_ref.shape[1]
    parts = per_dev // 8
    per_group = ROWS // per_dev
    groups = devices // per_group
    group = me // per_group

    barrier = pltpu.get_barrier_semaphore()

    def greet(k, carry):
        there = lax.rem(me + k, devices)
        pl.semaphore_signal(barrier, inc=1, device_id={"src": there}, device_id_type=MESH)
        return carry

    lax.fori_loop(1, devices, greet, 0)

    lane = lax.broadcasted_iota(jnp.int32, (8, 128), 1)
    lane_group = lane // 32
    eight = lax.broadcasted_iota(jnp.int32, (8, per_dev), 0)
    coords = jnp.where(eight == 0, uvw_ref[0:1, :], 0.0)
    coords = jnp.where(eight == 1, uvw_ref[1:2, :], coords)
    coords = jnp.where(eight == 2, uvw_ref[2:3, :], coords)
    coords = jnp.concatenate([coords] * 16, 0).T
    features = []
    for c in range(chans):
        size, angle = polar(jones_ref[c, 0], jones_ref[c, 1])
        features += [-angle, (2.0 * LEAD * LEAD) * size]
    features = jnp.concatenate(features, 0).T

    def spread(pieces):
        total = pieces[0]
        for index, piece in enumerate(pieces[1:], 1):
            total = jnp.where(lane_group == index, piece, total)
        return total

    own_coords = spread([coords[8 * q : 8 * q + 8] for q in range(parts)])
    for c in range(chans):
        freq_ratio = 1.0 + 0.002 * channel_ref[c].astype(jnp.float32)
        pieces = [features[8 * q : 8 * q + 8] for q in range(parts)]
        pieces = [
            pltpu.roll(piece, (32 * (q - c)) % 128, 1) if q != c else piece
            for q, piece in enumerate(pieces)
        ]
        st_send[c, 0:8, :] = spread(pieces)
        st_send[c, 8:16, :] = own_coords * freq_ratio
    clusters = cluster_ref[...].astype(jnp.float32)
    for c in range(chans):
        so_send[c, 0:2, :] = position_ref[...]
        so_send[c, 2:3, :] = clusters
        so_send[c, 3:4, :] = flux_ref[c : c + 1, :]
    st_recv[me] = st_send[rank]
    so_recv[rank] = so_send[rank]

    pl.semaphore_wait(barrier, devices - 1)

    def source_copy(there_rank, slot):
        return pltpu.make_async_remote_copy(
            src_ref=so_send.at[there_rank],
            dst_ref=so_recv.at[slot],
            send_sem=so_sent.at[there_rank],
            recv_sem=so_came.at[slot],
            device_id={"src": plane * chans + there_rank},
            device_id_type=MESH,
        )

    def station_copy(there, slot):
        return pltpu.make_async_remote_copy(
            src_ref=st_send.at[lax.rem(there, chans)],
            dst_ref=st_recv.at[slot],
            send_sem=st_sent.at[there],
            recv_sem=st_came.at[slot],
            device_id={"src": there},
            device_id_type=MESH,
        )

    def result_copy(there, slot):
        return pltpu.make_async_remote_copy(
            src_ref=rs_send.at[there],
            dst_ref=rs_recv.at[slot],
            send_sem=rs_sent.at[there],
            recv_sem=rs_came.at[slot],
            device_id={"src": there},
            device_id_type=MESH,
        )

    for k in range(1, chans):
        there = lax.rem(rank + k, chans)
        source_copy(there, rank).start()
        station_copy(plane * chans + there, me).start()

    def send_stations(k, carry):
        there = nearest_first(plane, k // chans, planes) * chans + lax.rem(k, chans)
        station_copy(there, me).start()
        return carry

    lax.fori_loop(chans, devices, send_stations, 0)

    eight = lax.broadcasted_iota(jnp.int32, (8, width), 0)
    kinds = lax.broadcasted_iota(jnp.int32, (dirs, width), 0).astype(jnp.float32)

    def make_features(block, slot):
        cols = slice(block * width, block * width + width)
        l_row, m_row = so_recv[slot, 0:1, :], so_recv[slot, 1:2, :]
        n_row = jnp.sqrt(1.0 - l_row * l_row - m_row * m_row) - 1.0
        rows = jnp.where(eight == 0, l_row, jnp.where(eight == 1, m_row, 0.0))
        rows = jnp.where(eight == 2, n_row, rows)
        first, second, third = three_parts(rows)
        onehot = jnp.where(kinds == so_recv[slot, 2:3, :], 1.0, 0.0).astype(jnp.bfloat16)
        for index in range(4):
            feats[16 * index : 16 * index + 16, cols] = onehot
        pairs = ((first, second), (third, first), (second, first), (third, second))
        for index, pair in enumerate(pairs):
            at = 64 + 16 * index
            feats[at : at + 16, cols] = jnp.concatenate(pair, 0).astype(jnp.bfloat16)

    make_features(0, rank)
    for k in range(1, chans):
        slot = lax.rem(rank + k, chans)
        source_copy(rank, slot).wait_recv()
        make_features(k, slot)

    wide_lane = lax.broadcasted_iota(jnp.int32, (16, 128), 1)
    is_size = jnp.logical_and(wide_lane < 64, lax.rem(wide_lane, 32) >= 16)
    lane_slot = lax.rem(lane, 32) // 8

    def predict(step, carry):
        index = nearest_first(group, step, groups)
        blocks = []
        for j in range(per_group):
            there = index * per_group + j

            @pl.when(there != me)
            def _():
                station_copy(me, there).wait_recv()

            payload = st_recv[there]
            head, tail, _ = three_parts(payload[0:8])
            first, second, third = three_parts(payload[8:16])
            left = jnp.where(lane_slot == 3, second, first)
            right = jnp.where(lax.rem(lane_slot, 2) == 0, second, third)
            for q in range(parts):
                pieces = [
                    pltpu.roll(piece, (32 * (g - q)) % 128, 1) if g != q else piece
                    for g, piece in enumerate((head, tail, left, right))
                ]
                blocks.append(spread(pieces))
        for pair in range(ROWS // 16):
            value = jnp.concatenate(blocks[2 * pair : 2 * pair + 2], 0)
            at = 16 * pair
            table[at : at + 16, :] = jnp.where(is_size, 0.0, value).astype(jnp.bfloat16)
            below = ROWS + at
            table[below : below + 16, :] = jnp.where(is_size, value, 0.0).astype(jnp.bfloat16)

        for chunk in range(chans * width // CHUNK):
            begin = chunk * CHUNK
            cols = slice(begin, begin + CHUNK)
            slot = lax.rem(rank + begin // width, chans)
            inner = slice(begin % width, begin % width + CHUNK)
            weight = so_recv[slot, 3:4, inner] * scale
            found = jnp.dot(table[...], feats[:, cols], preferred_element_type=jnp.float32)
            for tile in range(ROWS // TS):
                turns = found[tile * TS : tile * TS + TS]
                double = found[ROWS + tile * TS : ROWS + tile * TS + TS]
                turns = turns - jnp.round(turns)
                square = turns * turns
                poly = square + jnp.float32(MONIC[2])
                poly = poly * square + jnp.float32(MONIC[1])
                poly = poly * square + jnp.float32(MONIC[0])
                sine = turns * poly
                square = sine * sine
                rest = ONE - square
                cosine = rest * lax.rsqrt(rest)
                real = double * (HALF - square)
                imag = (double * sine) * cosine
                at = index * (ROWS // TS) + tile
                plain[at, 0:TS, cols] = real.astype(jnp.bfloat16)
                plain[at, TS : 2 * TS, cols] = imag.astype(jnp.bfloat16)
                weighted[at, 0:TS, cols] = (real * weight).astype(jnp.bfloat16)
                weighted[at, TS : 2 * TS, cols] = (imag * weight).astype(jnp.bfloat16)
        return carry

    lax.fori_loop(0, groups, predict, 0)

    contract = (((1,), (1,)), ((), ()))

    def turned(value, shift):
        return pltpu.roll(value, (32 * shift) % 128, 1) if shift % 4 else value

    def owner_at(k):
        step = planes - 1 - k // chans
        return nearest_first(plane, step, planes) * chans + lax.rem(rank + 1 + k, chans)

    def send_result(there):
        @pl.when(there != me)
        def _():
            result_copy(there, me).start()

    def products(step, carry):
        for j in range(chans):
            k = step * chans + j
            owner = owner_at(k)
            left = weighted[tile_ref[0, owner]]
            right = plain[tile_ref[1, owner]]
            both = jnp.concatenate([right, right], 0)
            found = lax.dot_general(left, both, contract, preferred_element_type=jnp.float32)
            reals, imags = [], []
            for q in range(4):
                upper = found[8 * q : 8 * q + 8]
                lower = found[TS + 8 * q : TS + 8 * q + 8]
                reals.append(turned(upper, q) + turned(lower, q - 1))
                imags.append(turned(lower, q) - turned(upper, q - 1))
            rs_send[owner, 0:8, :] = spread(reals)
            rs_send[owner, 8:16, :] = spread(imags)
            if j:
                send_result(owner_at(k - 1))
            else:

                @pl.when(step > 0)
                def _():
                    send_result(owner_at(k - 1))

        return carry

    lax.fori_loop(0, planes, products, 0)

    def take(k, carry):
        there = lax.rem(me + k, devices)
        result_copy(me, there).wait_recv()
        return carry

    rs_recv[me] = rs_send[me]
    lax.fori_loop(1, devices, take, 0)

    same = tile_ref[0, me] == tile_ref[1, me]
    row = lax.broadcasted_iota(jnp.int32, (8, 128), 0)
    diagonal = row + 8 * lane_group == lax.rem(lane, 32)
    clear = jnp.logical_and(diagonal, same)
    for c in range(chans):
        total = rs_recv[c]
        for other in range(1, planes):
            total = total + rs_recv[other * chans + c]
        for part in range(2):
            value = jnp.where(clear, 0.0, total[8 * part : 8 * part + 8])
            for i in range(TS):
                out_ref[0, c, part : part + 1, i * TS : i * TS + TS] = value[
                    i % 8 : i % 8 + 1, i // 8 * TS : i // 8 * TS + TS
                ]

    def finish(k, carry):
        there = lax.rem(me + k, devices)
        station_copy(there, me).wait_send()
        result_copy(there, me).wait_send()
        return carry

    lax.fori_loop(1, devices, finish, 0)
    for k in range(1, chans):
        source_copy(lax.rem(rank + k, chans), rank).wait_send()


def on_device(positions, flux, cluster, jones, station_uvw, channels, tile_map):
    width = positions.shape[1]
    devices = lax.axis_size("src")
    scale = 1.0 / math.sqrt(width * devices)
    chans, _, dirs, per_dev = jones.shape
    tiles = devices * per_dev // TS

    vmem = pl.BlockSpec(memory_space=pltpu.VMEM)
    return pl.pallas_call(
        functools.partial(kernel, devices, chans, dirs, scale),
        out_shape=jax.ShapeDtypeStruct((1, chans, 2, TS * TS), jnp.float32),
        in_specs=[pl.BlockSpec(memory_space=pltpu.SMEM)] * 2 + [vmem] * 5,
        out_specs=vmem,
        scratch_shapes=[
            pltpu.VMEM((chans, 16, 128), jnp.float32),
            pltpu.VMEM((devices, 16, 128), jnp.float32),
            pltpu.VMEM((chans, 4, width), jnp.float32),
            pltpu.VMEM((chans, 4, width), jnp.float32),
            pltpu.VMEM((2 * ROWS, 128), jnp.bfloat16),
            pltpu.VMEM((128, chans * width), jnp.bfloat16),
            pltpu.VMEM((tiles, 2 * TS, chans * width), jnp.bfloat16),
            pltpu.VMEM((tiles, 2 * TS, chans * width), jnp.bfloat16),
            pltpu.VMEM((devices, 16, 128), jnp.float32),
            pltpu.VMEM((devices, 16, 128), jnp.float32),
            pltpu.SemaphoreType.DMA((devices,)),
            pltpu.SemaphoreType.DMA((devices,)),
            pltpu.SemaphoreType.DMA((chans,)),
            pltpu.SemaphoreType.DMA((chans,)),
            pltpu.SemaphoreType.DMA((devices,)),
            pltpu.SemaphoreType.DMA((devices,)),
        ],
        compiler_params=pltpu.CompilerParams(collective_id=0, has_side_effects=True),
    )(tile_map.T, channels, positions, flux, cluster[None], jones, station_uvw)


def solution(mesh):
    in_specs = (
        P(None, ("group", "src")),
        P(None, ("group", "src")),
        P(("group", "src")),
        P(None, None, None, ("group", "src")),
        P(None, ("group", "src")),
        P("group"),
        P("group", None),
    )
    out_specs = P(("group", "src"), None, None, None)
    return jax.shard_map(
        on_device, mesh=mesh, in_specs=in_specs, out_specs=out_specs, check_vma=False
    )
```

time: 36.2 us -> 36.1 us (level)
  the two profiles are of different devices: /device:TPU:29 before, /device:TPU:0 now
where the time goes in v1:
time: 36.1 us; the launch traced here: 35.8 us
  Pallas kernels  34.4 us (95%)
  local copies, waits for them, and re-layouts  1.38 us (4%)
    pallas_call x1, Pallas kernels, on_device(): pl.pallas_call(functools.partial(kernel, devices, chans, dirs, scale), ou...  34.4 us
    unnamed x1, local copies, waits for them, and re-layouts  1.38 us

profile of v1, /device:TPU:0, one launch (start us, length us, event | category | flops | bytes accessed | tf_op | source)
XLA Modules:
  0.0 35.8 jit_solution(8759787303471919374)
XLA Ops:
  0.0 34.4 %shard_map.73 = f32[1,4,2,1024]{3,2,1,0:T(2,128)} custom-call(s32[2,16]{1,0:T(2,128)} %bitcast.3, s32[4]{0:T(128)} %channel_ref.1, f32[2,1024]{1,0:T(2,128)} %position_ref.1, f32[4,1024]{1,0:T(4,128)} %flux_ref.1, s32[1,1024]{1,0:T(1,128)} %bitcast.2, f32[4,2,16,32]{3,2,1,0:T(8,128)} %jones_ref.1, f32[3,32]{1,0:T(4,128)} %uvw_ref.1), custom_call_target="tpu_custom_call" | custom-call | tf_op jit(solution)/shard_map/pallas_call | solution.py:368
  34.4 1.4 %copy.9 = f32[1,4,2,1024]{3,2,1,0:T(2,128)} copy(f32[1,4,2,1024]{3,2,1,0:T(2,128)} %shard_map.73) | data formatting | bytes 65536

commit v2 on v1

--- a/solution.py
+++ b/solution.py
@@ -69,6 +69,14 @@
     chans,
     dirs,
     scale,
+    tile_in,
+    channel_in,
+    position_in,
+    flux_in,
+    cluster_in,
+    jones_in,
+    uvw_in,
+    out_ref,
     tile_ref,
     channel_ref,
     position_ref,
@@ -76,7 +84,6 @@
     cluster_ref,
     jones_ref,
     uvw_ref,
-    out_ref,
     st_send,
     st_recv,
     so_send,
@@ -85,6 +92,7 @@
     feats,
     plain,
     weighted,
+    prods,
     rs_send,
     rs_recv,
     st_sent,
@@ -93,6 +101,7 @@
     so_came,
     rs_sent,
     rs_came,
+    loaded,
 ):
     me = lax.axis_index("src")
     rank = lax.rem(me, chans)
@@ -113,6 +122,25 @@
         return carry
 
     lax.fori_loop(1, devices, greet, 0)
+
+    loads = [
+        pltpu.make_async_copy(source, target, loaded.at[index])
+        for index, (source, target) in enumerate(
+            (
+                (jones_in, jones_ref),
+                (uvw_in, uvw_ref),
+                (channel_in, channel_ref),
+                (position_in, position_ref),
+                (flux_in, flux_ref),
+                (cluster_in, cluster_ref),
+                (tile_in, tile_ref),
+            )
+        )
+    ]
+    for load in loads:
+        load.start()
+    for load in loads:
+        load.wait()
 
     lane = lax.broadcasted_iota(jnp.int32, (8, 128), 1)
     lane_group = lane // 32
@@ -199,7 +227,6 @@
     kinds = lax.broadcasted_iota(jnp.int32, (dirs, width), 0).astype(jnp.float32)
 
     def make_features(block, slot):
-        cols = slice(block * width, block * width + width)
         l_row, m_row = so_recv[slot, 0:1, :], so_recv[slot, 1:2, :]
         n_row = jnp.sqrt(1.0 - l_row * l_row - m_row * m_row) - 1.0
         rows = jnp.where(eight == 0, l_row, jnp.where(eight == 1, m_row, 0.0))
@@ -207,11 +234,11 @@
         first, second, third = three_parts(rows)
         onehot = jnp.where(kinds == so_recv[slot, 2:3, :], 1.0, 0.0).astype(jnp.bfloat16)
         for index in range(4):
-            feats[16 * index : 16 * index + 16, cols] = onehot
+            feats[block, 16 * index : 16 * index + 16, :] = onehot
         pairs = ((first, second), (third, first), (second, first), (third, second))
         for index, pair in enumerate(pairs):
             at = 64 + 16 * index
-            feats[at : at + 16, cols] = jnp.concatenate(pair, 0).astype(jnp.bfloat16)
+            feats[block, at : at + 16, :] = jnp.concatenate(pair, 0).astype(jnp.bfloat16)
 
     make_features(0, rank)
     for k in range(1, chans):
@@ -223,7 +250,7 @@
     is_size = jnp.logical_and(wide_lane < 64, lax.rem(wide_lane, 32) >= 16)
     lane_slot = lax.rem(lane, 32) // 8
 
-    def predict(step, carry):
+    def make_table(step):
         index = nearest_first(group, step, groups)
         blocks = []
         for j in range(per_group):
@@ -247,17 +274,19 @@
         for pair in range(ROWS // 16):
             value = jnp.concatenate(blocks[2 * pair : 2 * pair + 2], 0)
             at = 16 * pair
-            table[at : at + 16, :] = jnp.where(is_size, 0.0, value).astype(jnp.bfloat16)
+            table[step, at : at + 16, :] = jnp.where(is_size, 0.0, value).astype(jnp.bfloat16)
             below = ROWS + at
-            table[below : below + 16, :] = jnp.where(is_size, value, 0.0).astype(jnp.bfloat16)
-
-        for chunk in range(chans * width // CHUNK):
-            begin = chunk * CHUNK
-            cols = slice(begin, begin + CHUNK)
-            slot = lax.rem(rank + begin // width, chans)
-            inner = slice(begin % width, begin % width + CHUNK)
-            weight = so_recv[slot, 3:4, inner] * scale
-            found = jnp.dot(table[...], feats[:, cols], preferred_element_type=jnp.float32)
+            table[step, below : below + 16, :] = jnp.where(is_size, value, 0.0).astype(
+                jnp.bfloat16
+            )
+
+    def predict(step, block, between=None):
+        index = nearest_first(group, step, groups)
+        slot = lax.rem(rank + block, chans)
+        for chunk in range(width // CHUNK):
+            cols = slice(chunk * CHUNK, chunk * CHUNK + CHUNK)
+            weight = so_recv[slot, 3:4, cols] * scale
+            found = jnp.dot(table[step], feats[block, :, cols], preferred_element_type=jnp.float32)
             for tile in range(ROWS // TS):
                 turns = found[tile * TS : tile * TS + TS]
                 double = found[ROWS + tile * TS : ROWS + tile * TS + TS]
@@ -273,55 +302,85 @@
                 real = double * (HALF - square)
                 imag = (double * sine) * cosine
                 at = index * (ROWS // TS) + tile
-                plain[at, 0:TS, cols] = real.astype(jnp.bfloat16)
-                plain[at, TS : 2 * TS, cols] = imag.astype(jnp.bfloat16)
-                weighted[at, 0:TS, cols] = (real * weight).astype(jnp.bfloat16)
-                weighted[at, TS : 2 * TS, cols] = (imag * weight).astype(jnp.bfloat16)
-        return carry
-
-    lax.fori_loop(0, groups, predict, 0)
+                plain[block][at, 0:TS, cols] = real.astype(jnp.bfloat16)
+                plain[block][at, TS : 2 * TS, cols] = imag.astype(jnp.bfloat16)
+                weighted[block][at, 0:TS, cols] = (real * weight).astype(jnp.bfloat16)
+                weighted[block][at, TS : 2 * TS, cols] = (imag * weight).astype(jnp.bfloat16)
+            if between is not None:
+                between(chunk)
 
     contract = (((1,), (1,)), ((), ()))
-
-    def turned(value, shift):
-        return pltpu.roll(value, (32 * shift) % 128, 1) if shift % 4 else value
+    prods[...] = jnp.zeros_like(prods)
 
     def owner_at(k):
         step = planes - 1 - k // chans
         return nearest_first(plane, step, planes) * chans + lax.rem(rank + 1 + k, chans)
 
-    def send_result(there):
-        @pl.when(there != me)
-        def _():
-            result_copy(there, me).start()
-
-    def products(step, carry):
+    def product(owner, block):
+        left = weighted[block][tile_ref[0, owner]]
+        right = plain[block][tile_ref[1, owner]]
+        return lax.dot_general(left, right, contract, preferred_element_type=jnp.float32)
+
+    make_table(0)
+    for block in range(chans):
+        predict(0, block)
+
+    def first_step(step, carry):
+        make_table(step)
+        predict(step, 0)
+        return carry
+
+    lax.fori_loop(1, groups, first_step, 0)
+
+    share = pl.cdiv(devices, groups - 1)
+
+    def far_step(block, step, carry):
+        def between(chunk):
+            pieces = width // CHUNK
+            for j in range(share * chunk // pieces, share * (chunk + 1) // pieces):
+                k = step * share + j
+                owner = owner_at(jnp.minimum(k, devices - 1))
+                prods[k, :, 0 : 2 * TS] += product(owner, block)
+
+        predict(step + 1, block + 1, between)
+        return carry
+
+    for block in range(chans - 1):
+        lax.fori_loop(0, groups - 1, functools.partial(far_step, block), 0)
+
+    def turned(value, shift):
+        return pltpu.roll(value, (32 * shift) % 128, 1) if shift % 4 else value
+
+    def finish_products(step):
+        for j in range(chans):
+            k = step * chans + j
+            prods[k, :, 0 : 2 * TS] += product(owner_at(k), chans - 1)
+
+    def pack(step):
         for j in range(chans):
             k = step * chans + j
             owner = owner_at(k)
-            left = weighted[tile_ref[0, owner]]
-            right = plain[tile_ref[1, owner]]
-            both = jnp.concatenate([right, right], 0)
-            found = lax.dot_general(left, both, contract, preferred_element_type=jnp.float32)
             reals, imags = [], []
             for q in range(4):
-                upper = found[8 * q : 8 * q + 8]
-                lower = found[TS + 8 * q : TS + 8 * q + 8]
+                upper = prods[k, 8 * q : 8 * q + 8]
+                lower = prods[k, TS + 8 * q : TS + 8 * q + 8]
                 reals.append(turned(upper, q) + turned(lower, q - 1))
                 imags.append(turned(lower, q) - turned(upper, q - 1))
             rs_send[owner, 0:8, :] = spread(reals)
             rs_send[owner, 8:16, :] = spread(imags)
-            if j:
-                send_result(owner_at(k - 1))
-            else:
-
-                @pl.when(step > 0)
-                def _():
-                    send_result(owner_at(k - 1))
-
-        return carry
-
-    lax.fori_loop(0, planes, products, 0)
+
+    def last_step(step, carry):
+        finish_products(step + 1)
+        pack(step)
+        for j in range(chans):
+            result_copy(owner_at(step * chans + j), me).start()
+        return carry
+
+    finish_products(0)
+    lax.fori_loop(0, planes - 1, last_step, 0)
+    pack(planes - 1)
+    for j in range(chans - 1):
+        result_copy(owner_at(devices - chans + j), me).start()
 
     def take(k, carry):
         there = lax.rem(me + k, devices)
@@ -364,21 +423,30 @@
     chans, _, dirs, per_dev = jones.shape
     tiles = devices * per_dev // TS
 
-    vmem = pl.BlockSpec(memory_space=pltpu.VMEM)
+    groups = devices * per_dev // ROWS
+    share = pl.cdiv(devices, groups - 1)
+    sides = [pltpu.VMEM((tiles, 2 * TS, width), jnp.bfloat16)] * chans
+    cluster = cluster[None]
+    tile_map = tile_map.T
+    smem = [pltpu.SMEM(array.shape, array.dtype) for array in (tile_map, channels)]
+    inputs = (positions, flux, cluster, jones, station_uvw)
     return pl.pallas_call(
         functools.partial(kernel, devices, chans, dirs, scale),
         out_shape=jax.ShapeDtypeStruct((1, chans, 2, TS * TS), jnp.float32),
-        in_specs=[pl.BlockSpec(memory_space=pltpu.SMEM)] * 2 + [vmem] * 5,
-        out_specs=vmem,
-        scratch_shapes=[
+        in_specs=[pl.BlockSpec(memory_space=pl.ANY)] * 7,
+        out_specs=pl.BlockSpec(memory_space=pltpu.VMEM),
+        scratch_shapes=smem
+        + [pltpu.VMEM(array.shape, array.dtype) for array in inputs]
+        + [
             pltpu.VMEM((chans, 16, 128), jnp.float32),
             pltpu.VMEM((devices, 16, 128), jnp.float32),
             pltpu.VMEM((chans, 4, width), jnp.float32),
             pltpu.VMEM((chans, 4, width), jnp.float32),
-            pltpu.VMEM((2 * ROWS, 128), jnp.bfloat16),
-            pltpu.VMEM((128, chans * width), jnp.bfloat16),
-            pltpu.VMEM((tiles, 2 * TS, chans * width), jnp.bfloat16),
-            pltpu.VMEM((tiles, 2 * TS, chans * width), jnp.bfloat16),
+            pltpu.VMEM((groups, 2 * ROWS, 128), jnp.bfloat16),
+            pltpu.VMEM((chans, 128, width), jnp.bfloat16),
+            sides,
+            sides,
+            pltpu.VMEM((share * (groups - 1), 2 * TS, 128), jnp.float32),
             pltpu.VMEM((devices, 16, 128), jnp.float32),
             pltpu.VMEM((devices, 16, 128), jnp.float32),
             pltpu.SemaphoreType.DMA((devices,)),
@@ -387,9 +455,10 @@
             pltpu.SemaphoreType.DMA((chans,)),
             pltpu.SemaphoreType.DMA((devices,)),
             pltpu.SemaphoreType.DMA((devices,)),
+            pltpu.SemaphoreType.DMA((7,)),
         ],
         compiler_params=pltpu.CompilerParams(collective_id=0, has_side_effects=True),
-    )(tile_map.T, channels, positions, flux, cluster[None], jones, station_uvw)
+    )(tile_map, channels, *inputs)
 
 
 def solution(mesh):

time: 36.1 us -> 27.6 us (0.76)
  Pallas kernels: 34.4 us -> 26 us
    pallas_call x1, Pallas kernels: 34.4 us -> 26 us  [on_device(): pl.pallas_call(functools.partial(kernel, devices, chans, dirs, scale), ou...]
where the time goes in v2:
time: 27.6 us; the launch traced here: 27.4 us
  Pallas kernels  26 us (94%)
  local copies, waits for them, and re-layouts  1.38 us (5%)
    pallas_call x1, Pallas kernels, on_device(): pl.pallas_call(functools.partial(kernel, devices, chans, dirs, scale), ou...  26 us
    unnamed x1, local copies, waits for them, and re-layouts  1.38 us

profile of v2, /device:TPU:0, one launch (start us, length us, event | category | flops | bytes accessed | tf_op | source)
XLA Modules:
  0.0 27.4 jit_solution(8842082532947868452)
XLA Ops:
  0.0 26.0 %shard_map.73 = f32[1,4,2,1024]{3,2,1,0:T(2,128)} custom-call(s32[2,16]{1,0:T(2,128)} %bitcast.3, s32[4]{0:T(128)} %channel_in.1, f32[2,1024]{1,0:T(2,128)} %position_in.1, f32[4,1024]{1,0:T(4,128)} %flux_in.1, s32[1,1024]{1,0:T(1,128)} %bitcast.2, f32[4,2,16,32]{3,2,1,0:T(8,128)} %jones_in.1, f32[3,32]{1,0:T(4,128)} %uvw_in.1), custom_call_target="tpu_custom_call" | custom-call | tf_op jit(solution)/shard_map/pallas_call | solution.py:433
  26.0 1.4 %copy.9 = f32[1,4,2,1024]{3,2,1,0:T(2,128)} copy(f32[1,4,2,1024]{3,2,1,0:T(2,128)} %shard_map.73) | data formatting | bytes 65536

commit v3 on v2

--- a/solution.py
+++ b/solution.py
@@ -116,13 +116,6 @@
 
     barrier = pltpu.get_barrier_semaphore()
 
-    def greet(k, carry):
-        there = lax.rem(me + k, devices)
-        pl.semaphore_signal(barrier, inc=1, device_id={"src": there}, device_id_type=MESH)
-        return carry
-
-    lax.fori_loop(1, devices, greet, 0)
-
     loads = [
         pltpu.make_async_copy(source, target, loaded.at[index])
         for index, (source, target) in enumerate(
@@ -139,6 +132,14 @@
     ]
     for load in loads:
         load.start()
+
+    def greet(k, carry):
+        there = lax.rem(me + k, devices)
+        pl.semaphore_signal(barrier, inc=1, device_id={"src": there}, device_id_type=MESH)
+        return carry
+
+    lax.fori_loop(1, devices, greet, 0)
+
     for load in loads:
         load.wait()
 
@@ -233,12 +234,13 @@
         rows = jnp.where(eight == 2, n_row, rows)
         first, second, third = three_parts(rows)
         onehot = jnp.where(kinds == so_recv[slot, 2:3, :], 1.0, 0.0).astype(jnp.bfloat16)
-        for index in range(4):
-            feats[block, 16 * index : 16 * index + 16, :] = onehot
+        pieces = [(16 * index, onehot) for index in range(4)]
         pairs = ((first, second), (third, first), (second, first), (third, second))
         for index, pair in enumerate(pairs):
-            at = 64 + 16 * index
-            feats[block, at : at + 16, :] = jnp.concatenate(pair, 0).astype(jnp.bfloat16)
+            pieces.append((64 + 16 * index, jnp.concatenate(pair, 0).astype(jnp.bfloat16)))
+        for at, piece in pieces:
+            for lanes in range(width // 128):
+                feats[block, lanes, at : at + 16, :] = piece[:, 128 * lanes : 128 * lanes + 128]
 
     make_features(0, rank)
     for k in range(1, chans):
@@ -250,16 +252,23 @@
     is_size = jnp.logical_and(wide_lane < 64, lax.rem(wide_lane, 32) >= 16)
     lane_slot = lax.rem(lane, 32) // 8
 
+    def await_group(step):
+        index = nearest_first(group, step, groups)
+        for j in range(per_group):
+            there = index * per_group + j
+            if step:
+                station_copy(me, there).wait_recv()
+            else:
+
+                @pl.when(there != me)
+                def _():
+                    station_copy(me, there).wait_recv()
+
     def make_table(step):
         index = nearest_first(group, step, groups)
         blocks = []
         for j in range(per_group):
             there = index * per_group + j
-
-            @pl.when(there != me)
-            def _():
-                station_copy(me, there).wait_recv()
-
             payload = st_recv[there]
             head, tail, _ = three_parts(payload[0:8])
             first, second, third = three_parts(payload[8:16])
@@ -286,7 +295,11 @@
         for chunk in range(width // CHUNK):
             cols = slice(chunk * CHUNK, chunk * CHUNK + CHUNK)
             weight = so_recv[slot, 3:4, cols] * scale
-            found = jnp.dot(table[step], feats[block, :, cols], preferred_element_type=jnp.float32)
+            begin = chunk * (CHUNK // 128)
+            wide = [feats[block, begin + index] for index in range(CHUNK // 128)]
+            found = jnp.dot(
+                table[step], jnp.concatenate(wide, 1), preferred_element_type=jnp.float32
+            )
             for tile in range(ROWS // TS):
                 turns = found[tile * TS : tile * TS + TS]
                 double = found[ROWS + tile * TS : ROWS + tile * TS + TS]
@@ -302,10 +315,18 @@
                 real = double * (HALF - square)
                 imag = (double * sine) * cosine
                 at = index * (ROWS // TS) + tile
-                plain[block][at, 0:TS, cols] = real.astype(jnp.bfloat16)
-                plain[block][at, TS : 2 * TS, cols] = imag.astype(jnp.bfloat16)
-                weighted[block][at, 0:TS, cols] = (real * weight).astype(jnp.bfloat16)
-                weighted[block][at, TS : 2 * TS, cols] = (imag * weight).astype(jnp.bfloat16)
+                results = (
+                    (plain[block], 0, real),
+                    (plain[block], TS, imag),
+                    (weighted[block], 0, real * weight),
+                    (weighted[block], TS, imag * weight),
+                )
+                for side, top, value in results:
+                    value = value.astype(jnp.bfloat16)
+                    for index_in in range(CHUNK // 128):
+                        side[at, begin + index_in, top : top + TS, :] = value[
+                            :, 128 * index_in : 128 * index_in + 128
+                        ]
             if between is not None:
                 between(chunk)
 
@@ -317,36 +338,32 @@
         return nearest_first(plane, step, planes) * chans + lax.rem(rank + 1 + k, chans)
 
     def product(owner, block):
-        left = weighted[block][tile_ref[0, owner]]
-        right = plain[block][tile_ref[1, owner]]
+        first, second = tile_ref[0, owner], tile_ref[1, owner]
+        lanes = range(width // 128)
+        left = jnp.concatenate([weighted[block][first, index] for index in lanes], 1)
+        right = jnp.concatenate([plain[block][second, index] for index in lanes], 1)
         return lax.dot_general(left, right, contract, preferred_element_type=jnp.float32)
 
+    await_group(0)
     make_table(0)
-    for block in range(chans):
+    for block in range(chans - 1):
         predict(0, block)
-
-    def first_step(step, carry):
-        make_table(step)
-        predict(step, 0)
-        return carry
-
-    lax.fori_loop(1, groups, first_step, 0)
-
-    share = pl.cdiv(devices, groups - 1)
-
-    def far_step(block, step, carry):
-        def between(chunk):
-            pieces = width // CHUNK
-            for j in range(share * chunk // pieces, share * (chunk + 1) // pieces):
-                k = step * share + j
-                owner = owner_at(jnp.minimum(k, devices - 1))
-                prods[k, :, 0 : 2 * TS] += product(owner, block)
-
-        predict(step + 1, block + 1, between)
-        return carry
+    for step in range(groups):
+        if step + 1 < groups:
+            await_group(step + 1)
+            make_table(step + 1)
+        predict(step, 0 if step else chans - 1)
+
+    slots = (groups - 1) * (width // CHUNK)
+
+    def between(block, turn):
+        for k in range(devices * turn // slots, devices * (turn + 1) // slots):
+            prods[k, :, 0 : 2 * TS] += product(owner_at(k), block)
 
     for block in range(chans - 1):
-        lax.fori_loop(0, groups - 1, functools.partial(far_step, block), 0)
+        for step in range(1, groups):
+            base = (step - 1) * (width // CHUNK)
+            predict(step, block + 1, lambda chunk: between(block, base + chunk))
 
     def turned(value, shift):
         return pltpu.roll(value, (32 * shift) % 128, 1) if shift % 4 else value
@@ -382,6 +399,16 @@
     for j in range(chans - 1):
         result_copy(owner_at(devices - chans + j), me).start()
 
+    def finish(k, carry):
+        there = lax.rem(me + k, devices)
+        station_copy(there, me).wait_send()
+        result_copy(there, me).wait_send()
+        return carry
+
+    lax.fori_loop(1, devices, finish, 0)
+    for k in range(1, chans):
+        source_copy(lax.rem(rank + k, chans), rank).wait_send()
+
     def take(k, carry):
         there = lax.rem(me + k, devices)
         result_copy(me, there).wait_recv()
@@ -394,26 +421,23 @@
     row = lax.broadcasted_iota(jnp.int32, (8, 128), 0)
     diagonal = row + 8 * lane_group == lax.rem(lane, 32)
     clear = jnp.logical_and(diagonal, same)
+    lines = lax.rem(row, 4) == lane_group
     for c in range(chans):
         total = rs_recv[c]
         for other in range(1, planes):
             total = total + rs_recv[other * chans + c]
         for part in range(2):
             value = jnp.where(clear, 0.0, total[8 * part : 8 * part + 8])
-            for i in range(TS):
-                out_ref[0, c, part : part + 1, i * TS : i * TS + TS] = value[
-                    i % 8 : i % 8 + 1, i // 8 * TS : i // 8 * TS + TS
-                ]
-
-    def finish(k, carry):
-        there = lax.rem(me + k, devices)
-        station_copy(there, me).wait_send()
-        result_copy(there, me).wait_send()
-        return carry
-
-    lax.fori_loop(1, devices, finish, 0)
-    for k in range(1, chans):
-        source_copy(lax.rem(rank + k, chans), rank).wait_send()
+            shifted = [turned(value, shift) for shift in range(4)]
+            for q in range(4):
+                piece = shifted[(4 - q) % 4]
+                for other in range(1, 4):
+                    piece = jnp.where(lane_group == other, shifted[(other - q) % 4], piece)
+                piece = jnp.where(lines, piece, 0.0)
+                for half in range(2):
+                    line = jnp.sum(piece[4 * half : 4 * half + 4], 0, keepdims=True)
+                    at = 128 * (2 * q + half)
+                    out_ref[0, c, part : part + 1, at : at + 128] = line
 
 
 def on_device(positions, flux, cluster, jones, station_uvw, channels, tile_map):
@@ -424,15 +448,14 @@
     tiles = devices * per_dev // TS
 
     groups = devices * per_dev // ROWS
-    share = pl.cdiv(devices, groups - 1)
-    sides = [pltpu.VMEM((tiles, 2 * TS, width), jnp.bfloat16)] * chans
+    sides = [pltpu.VMEM((tiles, width // 128, 2 * TS, 128), jnp.bfloat16)] * chans
     cluster = cluster[None]
     tile_map = tile_map.T
     smem = [pltpu.SMEM(array.shape, array.dtype) for array in (tile_map, channels)]
     inputs = (positions, flux, cluster, jones, station_uvw)
     return pl.pallas_call(
         functools.partial(kernel, devices, chans, dirs, scale),
-        out_shape=jax.ShapeDtypeStruct((1, chans, 2, TS * TS), jnp.float32),
+        out_shape=pltpu.VMEM((1, chans, 2, TS * TS), jnp.float32),
         in_specs=[pl.BlockSpec(memory_space=pl.ANY)] * 7,
         out_specs=pl.BlockSpec(memory_space=pltpu.VMEM),
         scratch_shapes=smem
@@ -443,10 +466,10 @@
             pltpu.VMEM((chans, 4, width), jnp.float32),
             pltpu.VMEM((chans, 4, width), jnp.float32),
             pltpu.VMEM((groups, 2 * ROWS, 128), jnp.bfloat16),
-            pltpu.VMEM((chans, 128, width), jnp.bfloat16),
+            pltpu.VMEM((chans, width // 128, 128, 128), jnp.bfloat16),
             sides,
             sides,
-            pltpu.VMEM((share * (groups - 1), 2 * TS, 128), jnp.float32),
+            pltpu.VMEM((devices, 2 * TS, 128), jnp.float32),
             pltpu.VMEM((devices, 16, 128), jnp.float32),
             pltpu.VMEM((devices, 16, 128), jnp.float32),
             pltpu.SemaphoreType.DMA((devices,)),

time: 27.6 us -> 23.4 us (0.85)
  Pallas kernels: 26 us -> 22.6 us
  local copies, waits for them, and re-layouts: 1.38 us -> 0.62 us
    pallas_call x1, Pallas kernels: 26 us -> 22.6 us  [on_device(): pl.pallas_call(functools.partial(kernel, devices, chans, dirs, scale), ou...]
    unnamed x1, local copies, waits for them, and re-layouts: 1.38 us -> 0.62 us
where the time goes in v3:
time: 23.4 us; the launch traced here: 23.3 us
  Pallas kernels  22.6 us (97%)
  local copies, waits for them, and re-layouts  0.62 us (3%)
    pallas_call x1, Pallas kernels, on_device(): pl.pallas_call(functools.partial(kernel, devices, chans, dirs, scale), ou...  22.6 us
    unnamed x1, local copies, waits for them, and re-layouts  0.62 us

profile of v3, /device:TPU:0, one launch (start us, length us, event | category | flops | bytes accessed | tf_op | source)
XLA Modules:
  0.0 23.3 jit_solution(10879685412951742162)
XLA Ops:
  0.0 22.6 %shard_map.73 = f32[1,4,2,1024]{3,2,1,0:T(2,128)S(1)} custom-call(s32[2,16]{1,0:T(2,128)} %bitcast.3, s32[4]{0:T(128)} %channel_in.1, f32[2,1024]{1,0:T(2,128)} %position_in.1, f32[4,1024]{1,0:T(4,128)} %flux_in.1, s32[1,1024]{1,0:T(1,128)} %bitcast.2, f32[4,2,16,32]{3,2,1,0:T(8,128)} %jones_in.1, f32[3,32]{1,0:T(4,128)} %uvw_in.1), custom_call_target="tpu_custom_call" | custom-call | tf_op jit(solution)/shard_map/pallas_call | solution.py:456
  22.6 0.6 %copy.9 = f32[1,4,2,1024]{3,2,1,0:T(2,128)} copy(f32[1,4,2,1024]{3,2,1,0:T(2,128)S(1)} %shard_map.73) | data formatting | bytes 65536

commit v4 on v3

--- a/solution.py
+++ b/solution.py
@@ -102,6 +102,7 @@
     rs_sent,
     rs_came,
     loaded,
+    ready,
 ):
     me = lax.axis_index("src")
     rank = lax.rem(me, chans)
@@ -113,6 +114,10 @@
     per_group = ROWS // per_dev
     groups = devices // per_group
     group = me // per_group
+
+    def slot_of(block):
+        outer = lax.rem(rank // 2 + block // 2, chans // 2)
+        return 2 * outer + lax.rem(rank + block, 2)
 
     barrier = pltpu.get_barrier_semaphore()
 
@@ -133,12 +138,23 @@
     for load in loads:
         load.start()
 
-    def greet(k, carry):
-        there = lax.rem(me + k, devices)
-        pl.semaphore_signal(barrier, inc=1, device_id={"src": there}, device_id_type=MESH)
+    def greet(there, carry):
+        @pl.when(there != me)
+        def _():
+            pl.semaphore_signal(barrier, inc=1, device_id={"src": there}, device_id_type=MESH)
+
         return carry
 
-    lax.fori_loop(1, devices, greet, 0)
+    lax.fori_loop(plane * chans, devices, greet, 0)
+    pl.semaphore_wait(barrier, plane * chans + chans - 1)
+
+    def answer(there, carry):
+        pl.semaphore_signal(
+            ready.at[plane], inc=1, device_id={"src": there}, device_id_type=MESH
+        )
+        return carry
+
+    lax.fori_loop(0, plane * chans, answer, 0)
 
     for load in loads:
         load.wait()
@@ -180,8 +196,6 @@
     st_recv[me] = st_send[rank]
     so_recv[rank] = so_send[rank]
 
-    pl.semaphore_wait(barrier, devices - 1)
-
     def source_copy(there_rank, slot):
         return pltpu.make_async_remote_copy(
             src_ref=so_send.at[there_rank],
@@ -213,16 +227,19 @@
         )
 
     for k in range(1, chans):
-        there = lax.rem(rank + k, chans)
+        there = slot_of(k)
         source_copy(there, rank).start()
         station_copy(plane * chans + there, me).start()
 
-    def send_stations(k, carry):
-        there = nearest_first(plane, k // chans, planes) * chans + lax.rem(k, chans)
+    def send_stations(there, carry):
         station_copy(there, me).start()
         return carry
 
-    lax.fori_loop(chans, devices, send_stations, 0)
+    def send_above(above, carry):
+        pl.semaphore_wait(ready.at[above], chans)
+        return lax.fori_loop(above * chans, above * chans + chans, send_stations, carry)
+
+    lax.fori_loop(0, plane * chans, send_stations, 0)
 
     eight = lax.broadcasted_iota(jnp.int32, (8, width), 0)
     kinds = lax.broadcasted_iota(jnp.int32, (dirs, width), 0).astype(jnp.float32)
@@ -242,20 +259,26 @@
             for lanes in range(width // 128):
                 feats[block, lanes, at : at + 16, :] = piece[:, 128 * lanes : 128 * lanes + 128]
 
-    make_features(0, rank)
-    for k in range(1, chans):
-        slot = lax.rem(rank + k, chans)
-        source_copy(rank, slot).wait_recv()
-        make_features(k, slot)
+    def take_source(block):
+        slot = slot_of(block)
+        if block:
+            source_copy(rank, slot).wait_recv()
+        make_features(block, slot)
+
+    take_source(0)
+    take_source(1)
 
     wide_lane = lax.broadcasted_iota(jnp.int32, (16, 128), 1)
     is_size = jnp.logical_and(wide_lane < 64, lax.rem(wide_lane, 32) >= 16)
     lane_slot = lax.rem(lane, 32) // 8
 
-    def await_group(step):
-        index = nearest_first(group, step, groups)
-        for j in range(per_group):
-            there = index * per_group + j
+    part_devices = per_group // 2
+    own_part = lax.rem(me, per_group) // part_devices
+
+    def await_part(step, part):
+        first_device = nearest_first(group, step, groups) * per_group + part * part_devices
+        for j in range(part_devices):
+            there = first_device + j
             if step:
                 station_copy(me, there).wait_recv()
             else:
@@ -264,12 +287,11 @@
                 def _():
                     station_copy(me, there).wait_recv()
 
-    def make_table(step):
-        index = nearest_first(group, step, groups)
+    def make_table(step, part):
+        first_device = nearest_first(group, step, groups) * per_group + part * part_devices
         blocks = []
-        for j in range(per_group):
-            there = index * per_group + j
-            payload = st_recv[there]
+        for j in range(part_devices):
+            payload = st_recv[first_device + j]
             head, tail, _ = three_parts(payload[0:8])
             first, second, third = three_parts(payload[8:16])
             left = jnp.where(lane_slot == 3, second, first)
@@ -280,29 +302,35 @@
                     for g, piece in enumerate((head, tail, left, right))
                 ]
                 blocks.append(spread(pieces))
-        for pair in range(ROWS // 16):
+        for pair in range(ROWS // 32):
             value = jnp.concatenate(blocks[2 * pair : 2 * pair + 2], 0)
             at = 16 * pair
-            table[step, at : at + 16, :] = jnp.where(is_size, 0.0, value).astype(jnp.bfloat16)
-            below = ROWS + at
-            table[step, below : below + 16, :] = jnp.where(is_size, value, 0.0).astype(
+            table[step, part, at : at + 16, :] = jnp.where(is_size, 0.0, value).astype(
                 jnp.bfloat16
             )
-
-    def predict(step, block, between=None):
-        index = nearest_first(group, step, groups)
-        slot = lax.rem(rank + block, chans)
+            below = ROWS // 2 + at
+            table[step, part, below : below + 16, :] = jnp.where(is_size, value, 0.0).astype(
+                jnp.bfloat16
+            )
+
+    def predict(step, block, part=None, between=None):
+        base = nearest_first(group, step, groups) * (ROWS // TS)
+        slot = slot_of(block)
+        if part is None:
+            rows = jnp.concatenate([table[step, 0], table[step, 1]], 0)
+        else:
+            rows = table[step, part]
+            base = base + part * (ROWS // TS // 2)
         for chunk in range(width // CHUNK):
             cols = slice(chunk * CHUNK, chunk * CHUNK + CHUNK)
             weight = so_recv[slot, 3:4, cols] * scale
             begin = chunk * (CHUNK // 128)
             wide = [feats[block, begin + index] for index in range(CHUNK // 128)]
-            found = jnp.dot(
-                table[step], jnp.concatenate(wide, 1), preferred_element_type=jnp.float32
-            )
-            for tile in range(ROWS // TS):
-                turns = found[tile * TS : tile * TS + TS]
-                double = found[ROWS + tile * TS : ROWS + tile * TS + TS]
+            found = jnp.dot(rows, jnp.concatenate(wide, 1), preferred_element_type=jnp.float32)
+            for tile in range(rows.shape[0] // (2 * TS)):
+                top = tile // 2 * ROWS + tile % 2 * TS
+                turns = found[top : top + TS]
+                double = found[top + ROWS // 2 : top + ROWS // 2 + TS]
                 turns = turns - jnp.round(turns)
                 square = turns * turns
                 poly = square + jnp.float32(MONIC[2])
@@ -314,7 +342,7 @@
                 cosine = rest * lax.rsqrt(rest)
                 real = double * (HALF - square)
                 imag = (double * sine) * cosine
-                at = index * (ROWS // TS) + tile
+                at = base + tile
                 results = (
                     (plain[block], 0, real),
                     (plain[block], TS, imag),
@@ -333,10 +361,6 @@
     contract = (((1,), (1,)), ((), ()))
     prods[...] = jnp.zeros_like(prods)
 
-    def owner_at(k):
-        step = planes - 1 - k // chans
-        return nearest_first(plane, step, planes) * chans + lax.rem(rank + 1 + k, chans)
-
     def product(owner, block):
         first, second = tile_ref[0, owner], tile_ref[1, owner]
         lanes = range(width // 128)
@@ -344,60 +368,88 @@
         right = jnp.concatenate([plain[block][second, index] for index in lanes], 1)
         return lax.dot_general(left, right, contract, preferred_element_type=jnp.float32)
 
-    await_group(0)
-    make_table(0)
+    await_part(0, own_part)
+    make_table(0, own_part)
+    predict(0, 0, own_part)
+    predict(0, 1, own_part)
+    lax.fori_loop(plane + 1, planes, send_above, 0)
+    await_part(0, 1 - own_part)
+    make_table(0, 1 - own_part)
+    for block in range(2, chans):
+        take_source(block)
+    predict(0, 0, 1 - own_part)
+    predict(0, 1, 1 - own_part)
+    for block in range(2, chans - 1):
+        predict(0, block)
+    queue = [(0, chans - 1)]
+    for step in range(1, groups):
+        for part in range(2):
+            await_part(step, part)
+        for part in range(2):
+            make_table(step, part)
+        for unit in queue + [(step, 0)]:
+            predict(*unit)
+        queue = [(1, 1)] if step == 1 else []
+    done = [[], [(1, 1)]] + [[]] * chans
+
     for block in range(chans - 1):
-        predict(0, block)
-    for step in range(groups):
-        if step + 1 < groups:
-            await_group(step + 1)
-            make_table(step + 1)
-        predict(step, 0 if step else chans - 1)
-
-    slots = (groups - 1) * (width // CHUNK)
-
-    def between(block, turn):
-        for k in range(devices * turn // slots, devices * (turn + 1) // slots):
-            prods[k, :, 0 : 2 * TS] += product(owner_at(k), block)
-
-    for block in range(chans - 1):
-        for step in range(1, groups):
-            base = (step - 1) * (width // CHUNK)
-            predict(step, block + 1, lambda chunk: between(block, base + chunk))
+        units = [(step, block + 1) for step in range(1, groups)]
+        units = [unit for unit in units if unit not in done[block + 1]]
+        slots = len(units) * (width // CHUNK)
+
+        def between(turn):
+            for owner in range(devices * turn // slots, devices * (turn + 1) // slots):
+                prods[owner, :, 0 : 2 * TS] += product(owner, block)
+
+        for index, unit in enumerate(units):
+            base = index * (width // CHUNK)
+            predict(*unit, between=lambda chunk: between(base + chunk))
 
     def turned(value, shift):
         return pltpu.roll(value, (32 * shift) % 128, 1) if shift % 4 else value
 
-    def finish_products(step):
-        for j in range(chans):
-            k = step * chans + j
-            prods[k, :, 0 : 2 * TS] += product(owner_at(k), chans - 1)
-
-    def pack(step):
-        for j in range(chans):
-            k = step * chans + j
-            owner = owner_at(k)
+    def finish_products(owners):
+        for owner in owners:
+            prods[owner, :, 0 : 2 * TS] += product(owner, chans - 1)
+
+    def pack(owners):
+        for owner in owners:
             reals, imags = [], []
             for q in range(4):
-                upper = prods[k, 8 * q : 8 * q + 8]
-                lower = prods[k, TS + 8 * q : TS + 8 * q + 8]
+                upper = prods[owner, 8 * q : 8 * q + 8]
+                lower = prods[owner, TS + 8 * q : TS + 8 * q + 8]
                 reals.append(turned(upper, q) + turned(lower, q - 1))
                 imags.append(turned(lower, q) - turned(upper, q - 1))
             rs_send[owner, 0:8, :] = spread(reals)
             rs_send[owner, 8:16, :] = spread(imags)
 
+    def send(owners):
+        for owner in owners:
+
+            @pl.when(owner != me)
+            def _():
+                result_copy(owner, me).start()
+
+    def owners_of(step):
+        return [step * chans + j for j in range(chans)]
+
     def last_step(step, carry):
-        finish_products(step + 1)
-        pack(step)
-        for j in range(chans):
-            result_copy(owner_at(step * chans + j), me).start()
+        finish_products(owners_of(step + 1))
+        pack(owners_of(step))
+        send(owners_of(step))
         return carry
 
-    finish_products(0)
-    lax.fori_loop(0, planes - 1, last_step, 0)
-    pack(planes - 1)
-    for j in range(chans - 1):
-        result_copy(owner_at(devices - chans + j), me).start()
+    early, late = owners_of(0)[: chans // 2], owners_of(0)[chans // 2 :]
+    finish_products(early)
+    pack(early)
+    send(early)
+    finish_products(late)
+    pack(late)
+    send(late)
+    finish_products(owners_of(1))
+    lax.fori_loop(1, planes - 1, last_step, 0)
+    pack(owners_of(planes - 1))
+    send(owners_of(planes - 1))
 
     def finish(k, carry):
         there = lax.rem(me + k, devices)
@@ -465,7 +517,7 @@
             pltpu.VMEM((devices, 16, 128), jnp.float32),
             pltpu.VMEM((chans, 4, width), jnp.float32),
             pltpu.VMEM((chans, 4, width), jnp.float32),
-            pltpu.VMEM((groups, 2 * ROWS, 128), jnp.bfloat16),
+            pltpu.VMEM((groups, 2, ROWS, 128), jnp.bfloat16),
             pltpu.VMEM((chans, width // 128, 128, 128), jnp.bfloat16),
             sides,
             sides,
@@ -479,6 +531,7 @@
             pltpu.SemaphoreType.DMA((devices,)),
             pltpu.SemaphoreType.DMA((devices,)),
             pltpu.SemaphoreType.DMA((7,)),
+            pltpu.SemaphoreType.REGULAR((devices // chans,)),
         ],
         compiler_params=pltpu.CompilerParams(collective_id=0, has_side_effects=True),
     )(tile_map, channels, *inputs)

time: 23.4 us -> 22.5 us (0.962)
  Pallas kernels: 22.6 us -> 21.8 us
    pallas_call x1, Pallas kernels: 22.6 us -> 21.8 us  [on_device(): pl.pallas_call(functools.partial(kernel, devices, chans, dirs, scale), ou...]
where the time goes in v4:
time: 22.5 us; the launch traced here: 22.4 us
  Pallas kernels  21.8 us (97%)
  local copies, waits for them, and re-layouts  0.62 us (3%)
    pallas_call x1, Pallas kernels, on_device(): pl.pallas_call(functools.partial(kernel, devices, chans, dirs, scale), ou...  21.8 us
    unnamed x1, local copies, waits for them, and re-layouts  0.62 us

profile of v4, /device:TPU:0, one launch (start us, length us, event | category | flops | bytes accessed | tf_op | source)
XLA Modules:
  0.0 22.4 jit_solution(17248491598269125322)
XLA Ops:
  0.0 21.8 %shard_map.73 = f32[1,4,2,1024]{3,2,1,0:T(2,128)S(1)} custom-call(s32[2,16]{1,0:T(2,128)} %bitcast.3, s32[4]{0:T(128)} %channel_in.1, f32[2,1024]{1,0:T(2,128)} %position_in.1, f32[4,1024]{1,0:T(4,128)} %flux_in.1, s32[1,1024]{1,0:T(1,128)} %bitcast.2, f32[4,2,16,32]{3,2,1,0:T(8,128)} %jones_in.1, f32[3,32]{1,0:T(4,128)} %uvw_in.1), custom_call_target="tpu_custom_call" | custom-call | tf_op jit(solution)/shard_map/pallas_call | solution.py:508
  21.8 0.6 %copy.9 = f32[1,4,2,1024]{3,2,1,0:T(2,128)} copy(f32[1,4,2,1024]{3,2,1,0:T(2,128)S(1)} %shard_map.73) | data formatting | bytes 65536

commit v5 on v4

--- a/solution.py
+++ b/solution.py
@@ -112,6 +112,7 @@
     per_dev = uvw_ref.shape[1]
     parts = per_dev // 8
     per_group = ROWS // per_dev
+    part_devices = per_group // 2
     groups = devices // per_group
     group = me // per_group
 
@@ -200,7 +201,7 @@
         return pltpu.make_async_remote_copy(
             src_ref=so_send.at[there_rank],
             dst_ref=so_recv.at[slot],
-            send_sem=so_sent.at[there_rank],
+            send_sem=so_sent.at[0],
             recv_sem=so_came.at[slot],
             device_id={"src": plane * chans + there_rank},
             device_id_type=MESH,
@@ -210,8 +211,8 @@
         return pltpu.make_async_remote_copy(
             src_ref=st_send.at[lax.rem(there, chans)],
             dst_ref=st_recv.at[slot],
-            send_sem=st_sent.at[there],
-            recv_sem=st_came.at[slot],
+            send_sem=st_sent.at[0],
+            recv_sem=st_came.at[slot // part_devices],
             device_id={"src": there},
             device_id_type=MESH,
         )
@@ -220,9 +221,19 @@
         return pltpu.make_async_remote_copy(
             src_ref=rs_send.at[there],
             dst_ref=rs_recv.at[slot],
-            send_sem=rs_sent.at[there],
-            recv_sem=rs_came.at[slot],
+            send_sem=rs_sent.at[0],
+            recv_sem=rs_came.at[0],
             device_id={"src": there},
+            device_id_type=MESH,
+        )
+
+    def several(buffer, count, sent, came):
+        return pltpu.make_async_remote_copy(
+            src_ref=buffer.at[pl.ds(0, count)],
+            dst_ref=buffer.at[pl.ds(0, count)],
+            send_sem=sent.at[0],
+            recv_sem=came,
+            device_id={"src": plane * chans + slot_of(1)},
             device_id_type=MESH,
         )
 
@@ -272,20 +283,13 @@
     is_size = jnp.logical_and(wide_lane < 64, lax.rem(wide_lane, 32) >= 16)
     lane_slot = lax.rem(lane, 32) // 8
 
-    part_devices = per_group // 2
     own_part = lax.rem(me, per_group) // part_devices
 
-    def await_part(step, part):
-        first_device = nearest_first(group, step, groups) * per_group + part * part_devices
-        for j in range(part_devices):
-            there = first_device + j
-            if step:
-                station_copy(me, there).wait_recv()
-            else:
-
-                @pl.when(there != me)
-                def _():
-                    station_copy(me, there).wait_recv()
+    def await_part(step, part, missing=0):
+        index = nearest_first(group, step, groups) * 2 + part
+        count = part_devices - missing
+        if count:
+            several(st_recv, count, st_sent, st_came.at[index]).wait_recv()
 
     def make_table(step, part):
         first_device = nearest_first(group, step, groups) * per_group + part * part_devices
@@ -368,7 +372,7 @@
         right = jnp.concatenate([plain[block][second, index] for index in lanes], 1)
         return lax.dot_general(left, right, contract, preferred_element_type=jnp.float32)
 
-    await_part(0, own_part)
+    await_part(0, own_part, 1)
     make_table(0, own_part)
     predict(0, 0, own_part)
     predict(0, 1, own_part)
@@ -451,23 +455,11 @@
     pack(owners_of(planes - 1))
     send(owners_of(planes - 1))
 
-    def finish(k, carry):
-        there = lax.rem(me + k, devices)
-        station_copy(there, me).wait_send()
-        result_copy(there, me).wait_send()
-        return carry
-
-    lax.fori_loop(1, devices, finish, 0)
-    for k in range(1, chans):
-        source_copy(lax.rem(rank + k, chans), rank).wait_send()
-
-    def take(k, carry):
-        there = lax.rem(me + k, devices)
-        result_copy(me, there).wait_recv()
-        return carry
-
+    several(st_recv, devices - 1, st_sent, st_came.at[0]).wait_send()
+    several(so_recv, chans - 1, so_sent, so_came.at[0]).wait_send()
+    several(rs_recv, devices - 1, rs_sent, rs_came.at[0]).wait_send()
     rs_recv[me] = rs_send[me]
-    lax.fori_loop(1, devices, take, 0)
+    several(rs_recv, devices - 1, rs_sent, rs_came.at[0]).wait_recv()
 
     same = tile_ref[0, me] == tile_ref[1, me]
     row = lax.broadcasted_iota(jnp.int32, (8, 128), 0)
@@ -524,12 +516,12 @@
             pltpu.VMEM((devices, 2 * TS, 128), jnp.float32),
             pltpu.VMEM((devices, 16, 128), jnp.float32),
             pltpu.VMEM((devices, 16, 128), jnp.float32),
-            pltpu.SemaphoreType.DMA((devices,)),
-            pltpu.SemaphoreType.DMA((devices,)),
+            pltpu.SemaphoreType.DMA((1,)),
+            pltpu.SemaphoreType.DMA((2 * groups,)),
+            pltpu.SemaphoreType.DMA((1,)),
             pltpu.SemaphoreType.DMA((chans,)),
-            pltpu.SemaphoreType.DMA((chans,)),
-            pltpu.SemaphoreType.DMA((devices,)),
-            pltpu.SemaphoreType.DMA((devices,)),
+            pltpu.SemaphoreType.DMA((1,)),
+            pltpu.SemaphoreType.DMA((1,)),
             pltpu.SemaphoreType.DMA((7,)),
             pltpu.SemaphoreType.REGULAR((devices // chans,)),
         ],

time: 22.5 us -> 22 us (0.978)
  Pallas kernels: 21.8 us -> 21.3 us
    pallas_call x1, Pallas kernels: 21.8 us -> 21.3 us  [on_device(): pl.pallas_call(functools.partial(kernel, devices, chans, dirs, scale), ou...]
where the time goes in v5:
time: 22 us; the launch traced here: 21.9 us
  Pallas kernels  21.3 us (97%)
  local copies, waits for them, and re-layouts  0.62 us (3%)
    pallas_call x1, Pallas kernels, on_device(): pl.pallas_call(functools.partial(kernel, devices, chans, dirs, scale), ou...  21.3 us
    unnamed x1, local copies, waits for them, and re-layouts  0.62 us

profile of v5, /device:TPU:0, one launch (start us, length us, event | category | flops | bytes accessed | tf_op | source)
XLA Modules:
  0.0 21.9 jit_solution(5186121399840249439)
XLA Ops:
  0.0 21.3 %shard_map.73 = f32[1,4,2,1024]{3,2,1,0:T(2,128)S(1)} custom-call(s32[2,16]{1,0:T(2,128)} %bitcast.3, s32[4]{0:T(128)} %channel_in.1, f32[2,1024]{1,0:T(2,128)} %position_in.1, f32[4,1024]{1,0:T(4,128)} %flux_in.1, s32[1,1024]{1,0:T(1,128)} %bitcast.2, f32[4,2,16,32]{3,2,1,0:T(8,128)} %jones_in.1, f32[3,32]{1,0:T(4,128)} %uvw_in.1), custom_call_target="tpu_custom_call" | custom-call | tf_op jit(solution)/shard_map/pallas_call | solution.py:500
  21.3 0.6 %copy.9 = f32[1,4,2,1024]{3,2,1,0:T(2,128)} copy(f32[1,4,2,1024]{3,2,1,0:T(2,128)S(1)} %shard_map.73) | data formatting | bytes 65536

commit v6 on v5

--- a/solution.py
+++ b/solution.py
@@ -162,11 +162,6 @@
 
     lane = lax.broadcasted_iota(jnp.int32, (8, 128), 1)
     lane_group = lane // 32
-    eight = lax.broadcasted_iota(jnp.int32, (8, per_dev), 0)
-    coords = jnp.where(eight == 0, uvw_ref[0:1, :], 0.0)
-    coords = jnp.where(eight == 1, uvw_ref[1:2, :], coords)
-    coords = jnp.where(eight == 2, uvw_ref[2:3, :], coords)
-    coords = jnp.concatenate([coords] * 16, 0).T
     features = []
     for c in range(chans):
         size, angle = polar(jones_ref[c, 0], jones_ref[c, 1])
@@ -179,7 +174,6 @@
             total = jnp.where(lane_group == index, piece, total)
         return total
 
-    own_coords = spread([coords[8 * q : 8 * q + 8] for q in range(parts)])
     for c in range(chans):
         freq_ratio = 1.0 + 0.002 * channel_ref[c].astype(jnp.float32)
         pieces = [features[8 * q : 8 * q + 8] for q in range(parts)]
@@ -188,7 +182,10 @@
             for q, piece in enumerate(pieces)
         ]
         st_send[c, 0:8, :] = spread(pieces)
-        st_send[c, 8:16, :] = own_coords * freq_ratio
+        st_send[c, 8:9, :] = jnp.zeros((1, 128), jnp.float32)
+        for axis in range(3):
+            place = slice(32 * axis, 32 * axis + per_dev)
+            st_send[c, 8:9, place] = uvw_ref[axis : axis + 1, :] * freq_ratio
     clusters = cluster_ref[...].astype(jnp.float32)
     for c in range(chans):
         so_send[c, 0:2, :] = position_ref[...]
@@ -291,21 +288,36 @@
         if count:
             several(st_recv, count, st_sent, st_came.at[index]).wait_recv()
 
+    axis_row = lax.broadcasted_iota(jnp.int32, (8, 128), 0)
+    from_device = lane // per_dev
+
     def make_table(step, part):
         first_device = nearest_first(group, step, groups) * per_group + part * part_devices
+        coords = jnp.zeros((8, 128), jnp.float32)
+        for j in range(part_devices):
+            line = jnp.broadcast_to(st_recv[first_device + j, 8:9, :], (8, 128))
+            begin = j * per_dev
+            lines = [
+                pltpu.roll(line, (begin - 32 * axis) % 128, 1) if begin != 32 * axis else line
+                for axis in range(3)
+            ]
+            value = jnp.where(axis_row == 1, lines[1], jnp.where(axis_row == 2, lines[2], 0.0))
+            value = jnp.where(axis_row == 0, lines[0], value)
+            coords = jnp.where(from_device == j, value, coords)
+        coords = jnp.concatenate([coords[:, : ROWS // 2]] * 16, 0).T
         blocks = []
         for j in range(part_devices):
-            payload = st_recv[first_device + j]
-            head, tail, _ = three_parts(payload[0:8])
-            first, second, third = three_parts(payload[8:16])
-            left = jnp.where(lane_slot == 3, second, first)
-            right = jnp.where(lax.rem(lane_slot, 2) == 0, second, third)
+            head, tail, _ = three_parts(st_recv[first_device + j, 0:8, :])
             for q in range(parts):
+                at = j * per_dev + 8 * q
+                first, second, third = three_parts(coords[at : at + 8])
+                left = jnp.where(lane_slot == 3, second, first)
+                right = jnp.where(lax.rem(lane_slot, 2) == 0, second, third)
                 pieces = [
                     pltpu.roll(piece, (32 * (g - q)) % 128, 1) if g != q else piece
-                    for g, piece in enumerate((head, tail, left, right))
+                    for g, piece in enumerate((head, tail))
                 ]
-                blocks.append(spread(pieces))
+                blocks.append(spread(pieces + [left, right]))
         for pair in range(ROWS // 32):
             value = jnp.concatenate(blocks[2 * pair : 2 * pair + 2], 0)
             at = 16 * pair
@@ -383,22 +395,25 @@
         take_source(block)
     predict(0, 0, 1 - own_part)
     predict(0, 1, 1 - own_part)
-    for block in range(2, chans - 1):
+    for block in range(2, chans):
         predict(0, block)
-    queue = [(0, chans - 1)]
+    before = {2: [(1, 1)], 3: []}
+    beside = {2: [(1, 2)], 3: [(2, 1)]}
+    early_units = [(1, 1), (1, 2), (2, 1)]
     for step in range(1, groups):
+        for unit in before.get(step, []):
+            predict(*unit)
         for part in range(2):
             await_part(step, part)
         for part in range(2):
             make_table(step, part)
-        for unit in queue + [(step, 0)]:
+        for unit in beside.get(step, []):
             predict(*unit)
-        queue = [(1, 1)] if step == 1 else []
-    done = [[], [(1, 1)]] + [[]] * chans
+        predict(step, 0)
 
     for block in range(chans - 1):
         units = [(step, block + 1) for step in range(1, groups)]
-        units = [unit for unit in units if unit not in done[block + 1]]
+        units = [unit for unit in units if unit not in early_units]
         slots = len(units) * (width // CHUNK)
 
         def between(turn):
@@ -505,8 +520,8 @@
         scratch_shapes=smem
         + [pltpu.VMEM(array.shape, array.dtype) for array in inputs]
         + [
-            pltpu.VMEM((chans, 16, 128), jnp.float32),
-            pltpu.VMEM((devices, 16, 128), jnp.float32),
+            pltpu.VMEM((chans, 9, 128), jnp.float32),
+            pltpu.VMEM((devices, 9, 128), jnp.float32),
             pltpu.VMEM((chans, 4, width), jnp.float32),
             pltpu.VMEM((chans, 4, width), jnp.float32),
             pltpu.VMEM((groups, 2, ROWS, 128), jnp.bfloat16),

time: 22 us -> 21 us (0.955)
  Pallas kernels: 21.3 us -> 20.2 us
    pallas_call x1, Pallas kernels: 21.3 us -> 20.2 us  [on_device(): pl.pallas_call(functools.partial(kernel, devices, chans, dirs, scale), ou...]
where the time goes in v6:
time: 21 us; the launch traced here: 20.9 us
  Pallas kernels  20.2 us (96%)
  local copies, waits for them, and re-layouts  0.62 us (3%)
    pallas_call x1, Pallas kernels, on_device(): pl.pallas_call(functools.partial(kernel, devices, chans, dirs, scale), ou...  20.2 us
    unnamed x1, local copies, waits for them, and re-layouts  0.62 us

profile of v6, /device:TPU:0, one launch (start us, length us, event | category | flops | bytes accessed | tf_op | source)
XLA Modules:
  0.0 20.9 jit_solution(10191720961820908215)
XLA Ops:
  0.0 20.2 %shard_map.73 = f32[1,4,2,1024]{3,2,1,0:T(2,128)S(1)} custom-call(s32[2,16]{1,0:T(2,128)} %bitcast.3, s32[4]{0:T(128)} %channel_in.1, f32[2,1024]{1,0:T(2,128)} %position_in.1, f32[4,1024]{1,0:T(4,128)} %flux_in.1, s32[1,1024]{1,0:T(1,128)} %bitcast.2, f32[4,2,16,32]{3,2,1,0:T(8,128)} %jones_in.1, f32[3,32]{1,0:T(4,128)} %uvw_in.1), custom_call_target="tpu_custom_call" | custom-call | tf_op jit(solution)/shard_map/pallas_call | solution.py:515
  20.2 0.6 %copy.9 = f32[1,4,2,1024]{3,2,1,0:T(2,128)} copy(f32[1,4,2,1024]{3,2,1,0:T(2,128)S(1)} %shard_map.73) | data formatting | bytes 65536

commit v7 on v6

--- a/solution.py
+++ b/solution.py
@@ -147,15 +147,6 @@
         return carry
 
     lax.fori_loop(plane * chans, devices, greet, 0)
-    pl.semaphore_wait(barrier, plane * chans + chans - 1)
-
-    def answer(there, carry):
-        pl.semaphore_signal(
-            ready.at[plane], inc=1, device_id={"src": there}, device_id_type=MESH
-        )
-        return carry
-
-    lax.fori_loop(0, plane * chans, answer, 0)
 
     for load in loads:
         load.wait()
@@ -193,6 +184,16 @@
         so_send[c, 3:4, :] = flux_ref[c : c + 1, :]
     st_recv[me] = st_send[rank]
     so_recv[rank] = so_send[rank]
+
+    pl.semaphore_wait(barrier, plane * chans + chans - 1)
+
+    def answer(there, carry):
+        pl.semaphore_signal(
+            ready.at[plane], inc=1, device_id={"src": there}, device_id_type=MESH
+        )
+        return carry
+
+    lax.fori_loop(0, plane * chans, answer, 0)
 
     def source_copy(there_rank, slot):
         return pltpu.make_async_remote_copy(
@@ -397,19 +398,16 @@
     predict(0, 1, 1 - own_part)
     for block in range(2, chans):
         predict(0, block)
-    before = {2: [(1, 1)], 3: []}
-    beside = {2: [(1, 2)], 3: [(2, 1)]}
-    early_units = [(1, 1), (1, 2), (2, 1)]
+    beside = {1: [], 2: [(1, 2)], 3: [(2, 0)]}
+    after = {1: [(1, 0), (1, 1)], 2: [], 3: [(3, 0)]}
+    early_units = [(1, 1), (1, 2)]
     for step in range(1, groups):
-        for unit in before.get(step, []):
-            predict(*unit)
         for part in range(2):
             await_part(step, part)
         for part in range(2):
             make_table(step, part)
-        for unit in beside.get(step, []):
+        for unit in beside[step] + after[step]:
             predict(*unit)
-        predict(step, 0)
 
     for block in range(chans - 1):
         units = [(step, block + 1) for step in range(1, groups)]

time: 21 us -> 21 us (level)
  no operation moved by 1% of the time
where the time goes in v7:
time: 21 us; the launch traced here: 20.8 us
  Pallas kernels  20.2 us (96%)
  local copies, waits for them, and re-layouts  0.62 us (3%)
    pallas_call x1, Pallas kernels, on_device(): pl.pallas_call(functools.partial(kernel, devices, chans, dirs, scale), ou...  20.2 us
    unnamed x1, local copies, waits for them, and re-layouts  0.62 us

profile of v7, /device:TPU:0, one launch (start us, length us, event | category | flops | bytes accessed | tf_op | source)
XLA Modules:
  0.0 20.8 jit_solution(16122173855516545914)
XLA Ops:
  0.0 20.2 %shard_map.73 = f32[1,4,2,1024]{3,2,1,0:T(2,128)S(1)} custom-call(s32[2,16]{1,0:T(2,128)} %bitcast.3, s32[4]{0:T(128)} %channel_in.1, f32[2,1024]{1,0:T(2,128)} %position_in.1, f32[4,1024]{1,0:T(4,128)} %flux_in.1, s32[1,1024]{1,0:T(1,128)} %bitcast.2, f32[4,2,16,32]{3,2,1,0:T(8,128)} %jones_in.1, f32[3,32]{1,0:T(4,128)} %uvw_in.1), custom_call_target="tpu_custom_call" | custom-call | tf_op jit(solution)/shard_map/pallas_call | solution.py:513
  20.2 0.6 %copy.9 = f32[1,4,2,1024]{3,2,1,0:T(2,128)} copy(f32[1,4,2,1024]{3,2,1,0:T(2,128)S(1)} %shard_map.73) | data formatting | bytes 65536
